TPU v7x, 512 devices: a whole 4x8x8 slice. The times are simulated.
512 devices in a mesh: seq: 64 (over x, z, core), head: 8 (over y).
Axes of the slice: x: 4, y: 8, z: 8, core: 2. Of those that a mesh axis runs over, the one named last changes fastest.
Arguments:
- queries: bfloat16 [16384, 4096], P('seq', 'head'), may hold values from -6 to 6
- keys: bfloat16 [16384, 4096], P('seq', 'head'), may hold values from -6 to 6
- values: bfloat16 [16384, 4096], P('seq', 'head'), may hold values from -6 to 6
- gate: bfloat16 [16384, 4096], P('seq', 'head'), may hold values from -6 to 6
- residual: bfloat16 [16384, 4096], P('seq', 'head'), may hold values from -40 to 40
- log_decay: float32 [16384, 32], P('seq', 'head'), may hold values from -1 to 0, as said below
- out_weight: bfloat16 [4096, 4096], P('seq', 'head'), may hold values from -0.09375 to 0.09375
- norm_gain: bfloat16 [4096], P('head'), may hold values from 0.099609375 to 1.8984375
- kv_weight: bfloat16 [4096, 2048], P('seq', 'head'), may hold values from -0.09375 to 0.09375
Outputs:
- cache_keys: bfloat16 [16384, 1024], P('seq', 'head')
- cache_values: bfloat16 [16384, 1024], P('seq', 'head')
Inputs may be any that keep to these rules, and one draw needn't show every extreme that they name: `log_decay`: every entry is negative.
All inputs are finite; a program needn't handle non-finite values.
Results may differ from a plain program's by a relative error of at most 0.015.
Values may be sent and summed in bfloat16 or wider, within the bound.
A program may use at most 64 MiB of HBM per device.

v0:
```python
import jax
import jax.numpy as jnp
from jax import lax
from jax.sharding import PartitionSpec as P

HIGHEST = lax.Precision.HIGHEST


def entering(part, axis, combine, identity):
    place = lax.axis_index(axis)
    gathered = jax.tree.map(lambda a: lax.all_gather(a, axis), part)
    state = jax.tree.map(lambda a, e: jnp.zeros_like(a) + jnp.asarray(e, a.dtype), part, identity)

    def one(step, state):
        return combine(
            state, jax.tree.map(lambda a: lax.dynamic_index_in_dim(a, step, 0, False), gathered)
        )

    return lax.fori_loop(0, place, one, state)


def local_retention(queries, keys, values, log_decay, block):
    tokens, heads, width = queries.shape
    count = tokens // block

    def to_blocks(array):
        return array.reshape((count, block) + array.shape[1:])

    lower = jnp.arange(block)[:, None] >= jnp.arange(block)[None, :]

    def advance(carry, inputs):
        state, offset = carry
        query_block, key_block, value_block, decay_block = inputs
        within = jnp.cumsum(decay_block, axis=0)
        spread = within[:, None, :] - within[None, :, :]
        factor = jnp.where(
            lower[:, :, None], jnp.exp(jnp.where(lower[:, :, None], spread, 0.0)), 0.0
        )
        scores = jnp.einsum(
            "ihd,jhd->hij", query_block, key_block, preferred_element_type=jnp.float32
        )
        weighted = scores * jnp.transpose(factor, (2, 0, 1))
        values_wide = value_block.astype(jnp.float32)
        intra = jnp.einsum("hij,jhd->ihd", weighted, values_wide, precision=HIGHEST)
        query_wide = query_block.astype(jnp.float32)
        carried = jnp.exp(within)[:, :, None] * jnp.einsum(
            "ihd,hde->ihe", query_wide, state, precision=HIGHEST
        )
        ending = within[-1]
        key_wide = key_block.astype(jnp.float32) * jnp.exp(ending[None, :] - within)[:, :, None]
        fresh = jnp.exp(ending)[:, None, None] * state + jnp.einsum(
            "jhd,jhe->hde", key_wide, values_wide, precision=HIGHEST
        )
        return ((fresh, offset + ending), (intra + carried, offset[None, :] + within))

    start = (jnp.zeros((heads, width, width), jnp.float32), jnp.zeros((heads,), jnp.float32))
    final, stacked = lax.scan(
        advance,
        start,
        (to_blocks(queries), to_blocks(keys), to_blocks(values), to_blocks(log_decay)),
    )
    return (
        stacked[0].reshape(tokens, heads, width),
        stacked[1].reshape(tokens, heads),
        final[0],
        final[1],
    )


def combine_states(earlier, later):
    return (earlier[0] * later[0], later[0][:, None, None] * earlier[1] + later[1])


def on_device(queries, keys, values, gate, residual, log_decay, out_weight, norm_gain, kv_weight):
    tokens = queries.shape[0]
    heads = log_decay.shape[1]
    width = queries.shape[1] // heads
    shaped = [array.reshape(tokens, heads, width) for array in (queries, keys, values)]
    partial_out, running, state, offset = local_retention(
        shaped[0], shaped[1], shaped[2], log_decay, min(512, tokens)
    )
    identity = (jnp.ones((heads,), jnp.float32), jnp.zeros((heads, width, width), jnp.float32))
    scan_decay, incoming = entering((jnp.exp(offset), state), "seq", combine_states, identity)
    retained = partial_out + jnp.exp(running)[:, :, None] * jnp.einsum(
        "thd,hde->the", shaped[0].astype(jnp.float32), incoming, precision=HIGHEST
    )
    scale = lax.rsqrt(jnp.mean(retained * retained, axis=2, keepdims=True) + 1e-06)
    mixed = (
        jax.nn.silu(gate.astype(jnp.float32)) * (retained * scale).reshape(tokens, heads * width)
    ).astype(jnp.bfloat16)
    all_heads = lax.all_gather(mixed, "head", axis=1, tiled=True)
    out_full, kv_full = (
        lax.all_gather(out_weight, "seq", axis=0, tiled=True),
        lax.all_gather(kv_weight, "seq", axis=0, tiled=True),
    )
    branch = jnp.dot(all_heads, out_full, preferred_element_type=jnp.float32)
    hidden = (residual.astype(jnp.float32) + branch).astype(jnp.bfloat16)
    wide = hidden.astype(jnp.float32)
    squares = lax.psum(jnp.sum(wide * wide, axis=1), "head")
    features = wide.shape[1] * lax.axis_size("head")
    inverse = lax.rsqrt(squares[:, None] / features + 1e-06)
    local_norm = (wide * inverse * norm_gain.astype(jnp.float32)[None, :]).astype(jnp.bfloat16)
    normalized = lax.all_gather(local_norm, "head", axis=1, tiled=True)
    projected = jnp.dot(normalized, kv_full, preferred_element_type=jnp.float32)
    cache_heads = kv_weight.shape[1] // (2 * width)
    arranged = projected.reshape(tokens, cache_heads, 2, width)
    cache_keys = arranged[:, :, 0, :].reshape(tokens, cache_heads * width).astype(jnp.bfloat16)
    cache_values = arranged[:, :, 1, :].reshape(tokens, cache_heads * width).astype(jnp.bfloat16)
    return (cache_keys, cache_values)


def solution(mesh):
    placed = (
        P("seq", "head"),
        P("seq", "head"),
        P("seq", "head"),
        P("seq", "head"),
        P("seq", "head"),
        P("seq", "head"),
        P("seq", "head"),
        P("head"),
        P("seq", "head"),
    )
    return jax.shard_map(
        on_device,
        mesh=mesh,
        in_specs=placed,
        out_specs=(P("seq", "head"), P("seq", "head")),
        check_vma=False,
    )
```

profile of v0, /device:TPU:2, one launch (start us, length us, event | category | flops | bytes accessed | tf_op | source)
XLA Modules:
  0.0 390.9 jit_solution(8764286394529594663)
XLA Ops:
  8.0 1.2 reduce-window.6
  9.8 1.1 copy.73
  10.9 2.0 convolution_add_fusion.1
  13.8 44.7 %all-gather.1 = f32[64,1,4]{2,1,0:T(1,128)S(1)} all-gather(f32[1,1,4]{2,1,0:T(1,128)S(1)} %bitcast.97), channel_id=1, replica_groups=mesh['seq'=64,'head'=8] {'seq'}, dimensions={0}, use_global_device_ids=true | all-gather | bytes 1040 | tf_op jit(solution)/shard_map/all_gather | solution.py:11
  59.4 63.1 %all-gather.16.cloned.1.call-done = f32[256,128,128]{2,1,0:T(8,128)} async-done(((f32[4,128,128]{2,1,0:T(8,128)}), f32[256,128,128]{2,1,0:T(8,128)}) %all-gather.16.cloned.1.call-update) | async-done | bytes 16777232 | tf_op jit(solution)/shard_map/all_gather | solution.py:11
  122.5 17.8 %while.3 = (s32[]{:T(128)}, f32[4,128,128]{2,1,0:T(8,128)S(1)}, s32[]{:T(128)}, f32[64,4]{1,0:T(8,128)S(1)}, f32[64,4,128,128]{3,2,1,0:T(8,128)}, /*index=5*/s32[]{:T(128)}, s32[]{:T(128)}, s32[]{:T(128)}) while((s32[]{:T(128)}, f32[4,128,128]{2,1,0:T(8,128)S(1)}, s32[]{:T(128)}, f32[64,4]{1,0:T(8,128)S(1)}, f32[64,4,128,128]{3,2,1,0:T(8,128)}, ...), condition=%wide.region_3.4_spmd, body=%wide.region_2.3_spmd.sunk | while | flops 131077 | bytes 786607 | solution.py:19
  122.6 1.1 bitcast_add_fusion.2
  123.7 1.1 bitcast_add_fusion.2
  124.8 1.1 bitcast_add_fusion.2
  125.9 1.1 bitcast_add_fusion.2
  127.0 1.1 bitcast_add_fusion.2
  128.1 1.1 bitcast_add_fusion.2
  129.2 1.1 bitcast_add_fusion.2
  130.4 1.1 bitcast_add_fusion.2
  137.0 1.1 bitcast_add_fusion.2
  138.1 1.1 bitcast_add_fusion.2
  139.2 1.1 bitcast_add_fusion.2
  143.4 64.4 %all-gather.10.cloned.1.call-done = bf16[4096,512]{1,0:T(8,128)(2,1)} async-done(((bf16[64,512]{1,0:T(8,128)(2,1)}), bf16[4096,512]{1,0:T(8,128)(2,1)}) %all-gather.10.cloned.1.call-update) | async-done | bytes 4194320 | tf_op jit(solution)/shard_map/all_gather | solution.py:93
  207.8 43.4 %all-gather.8.cloned.1.call-done = bf16[256,4096]{1,0:T(8,128)(2,1)} async-done(((bf16[256,512]{1,0:T(8,128)(2,1)}), bf16[256,4096]{1,0:T(8,128)(2,1)}) %all-gather.8.cloned.1.call-update) | async-done | bytes 2097168 | tf_op jit(solution)/shard_map/all_gather | solution.py:91
  251.2 4.2 %multiply_reduce_fusion = (f32[256]{0:T(256)S(1)}, f32[256,512]{1,0:T(8,128)S(1)}) fusion(bf16[256,4096]{1,0:T(8,128)(2,1)} %all-gather.8.cloned.1.call-done, bf16[4096,512]{1,0:T(8,128)(2,1)} %all-gather.10.cloned.1.call-done, bf16[256,512]{1,0:T(8,128)(2,1)S(1)} %copy-done.4), kind=kOutput, calls=%fused_computation.22 | convolution fusion | flops 1074528000 | bytes 7078912 | tf_op jit(solution)/shard_map/dot_general | solution.py:96
  255.3 16.2 %psum.7 = f32[256]{0:T(256)S(1)} all-reduce(f32[256]{0:T(256)S(1)} %get-tuple-element.97), channel_id=1, replica_groups=mesh['seq'=64,'head'=8] {'head'}, use_global_device_ids=true, to_apply=%region_6.7 | all-reduce | flops 256 | bytes 2048 | tf_op jit(solution)/shard_map/psum | solution.py:99
  272.4 63.8 %all-gather.14.cloned.1.call-done = bf16[4096,256]{1,0:T(8,128)(2,1)} async-done(((bf16[64,256]{1,0:T(8,128)(2,1)}), bf16[4096,256]{1,0:T(8,128)(2,1)}) %all-gather.14.cloned.1.call-update) | async-done | bytes 2097168 | tf_op jit(solution)/shard_map/all_gather | solution.py:94
  336.2 43.6 %all-gather.12.cloned.1.call-done = bf16[256,4096]{1,0:T(8,128)(2,1)} async-done(((bf16[256,512]{1,0:T(8,128)(2,1)}), bf16[256,4096]{1,0:T(8,128)(2,1)}) %all-gather.12.cloned.1.call-update) | async-done | bytes 2097168 | tf_op jit(solution)/shard_map/all_gather | solution.py:103
  379.8 3.1 convolution_convert_fusion
  (68 shorter events, 13.8 us)
Async XLA Ops:
  7.2 51.4 %copy-start = (bf16[256,512]{1,0:T(8,128)(2,1)S(1)}, bf16[256,512]{1,0:T(8,128)(2,1)}, u32[]{:S(2)}) copy-start(bf16[256,512]{1,0:T(8,128)(2,1)} %param.11) | copy-start | bytes 786436
  7.2 115.3 %all-gather.16.cloned.1.call-start = ((), (), s32[]{:S(2)}) async-start(), calls=%async_computation.4 | async-start | bytes 17039360 | tf_op jit(solution)/shard_map/all_gather | solution.py:11
  13.0 194.8 %all-gather.10.cloned.1.call-start = ((), (), s32[]{:S(2)}) async-start(), calls=%async_computation.1 | async-start | bytes 4259840 | tf_op jit(solution)/shard_map/all_gather | solution.py:93
  13.8 237.4 %all-gather.8.cloned.1.call-start = ((), (), s32[]{:S(2)}) async-start(), calls=%async_computation | async-start | bytes 2359296 | tf_op jit(solution)/shard_map/all_gather | solution.py:91
  122.5 18.2 %copy-start.1 = (bf16[256,512]{1,0:T(8,128)(2,1)S(1)}, bf16[256,512]{1,0:T(8,128)(2,1)}, u32[]{:S(2)}) copy-start(bf16[256,512]{1,0:T(8,128)(2,1)} %param.13) | copy-start | bytes 786436
  140.8 1.1 copy-start.2
  141.5 1.8 copy-start.3
  141.5 109.7 %copy-start.4 = (bf16[256,512]{1,0:T(8,128)(2,1)S(1)}, bf16[256,512]{1,0:T(8,128)(2,1)}, u32[]{:S(2)}) copy-start(bf16[256,512]{1,0:T(8,128)(2,1)} %param.15) | copy-start | bytes 786436
  142.7 193.4 %all-gather.14.cloned.1.call-start = ((), (), s32[]{:S(2)}) async-start(), calls=%async_computation.3 | async-start | bytes 2129920 | tf_op jit(solution)/shard_map/all_gather | solution.py:94
  143.3 236.5 %all-gather.12.cloned.1.call-start = ((), (), s32[]{:S(2)}) async-start(), calls=%async_computation.2 | async-start | bytes 2359296 | tf_op jit(solution)/shard_map/all_gather | solution.py:103
Sparse Core Ops, SparseCore 0:
  13.1 109.3 all-gather.15
  125.8 81.8 all-gather.9
  209.9 41.2 all-gather.7
  254.4 81.7 all-gather.13
  338.1 41.6 all-gather.11
where the time goes:
time: 393 us; the launch traced here: 391 us
  waiting for transfers between devices  280 us (71%)
  blocking collectives  60.9 us (15%)
  other arithmetic  20.2 us (5%)
  between operations  14 us (4%)
  matrix products  11.3 us (3%)
  local copies, waits for them, and re-layouts  4.19 us (1%)
    all_gather x1, waiting for transfers between devices, on_device(): lax.all_gather(out_weight, 'seq', axis=0, tiled=True)  64.4 us
    all_gather x1, waiting for transfers between devices, on_device(): lax.all_gather(kv_weight, 'seq', axis=0, tiled=True)  63.8 us
    all_gather x1, waiting for transfers between devices, entering(): gathered = jax.tree.map(lambda a: lax.all_gather(a, axis), part)  63.1 us
    all_gather x1, blocking collectives, entering(): gathered = jax.tree.map(lambda a: lax.all_gather(a, axis), part)  44.7 us
    all_gather x1, waiting for transfers between devices, on_device(): normalized = lax.all_gather(local_norm, 'head', axis=1, tiled=True)  43.6 us
    all_gather x1, waiting for transfers between devices, on_device(): all_heads = lax.all_gather(mixed, 'head', axis=1, tiled=True)  43.4 us
    add x16, other arithmetic, combine_states(): later[0][:, None, None] * earlier[1] + later[1]  17 us
    psum x1, blocking collectives, on_device(): squares = lax.psum(jnp.sum(wide * wide, axis=1), 'head')  16.2 us
  transfers between devices with their start and end apart: 5, of which 5 were waited for; matrix products, arithmetic and copies ran while one was open for 6% of the time, Pallas kernels for 0%

commit v1 on v0

--- a/solution.py
+++ b/solution.py
@@ -88,7 +88,14 @@
     mixed = (
         jax.nn.silu(gate.astype(jnp.float32)) * (retained * scale).reshape(tokens, heads * width)
     ).astype(jnp.bfloat16)
-    all_heads = lax.all_gather(mixed, "head", axis=1, tiled=True)
+    size = lax.axis_size("head")
+    right = [(i, (i + 1) % size) for i in range(size)]
+    pieces = [mixed]
+    for stride in range(1, size):
+        pieces = [lax.ppermute(pieces[0], "head", right), *pieces]
+    out = jnp.concatenate(pieces, axis=1)
+    places = (lax.axis_index("head") + 1) * pieces[-1].shape[1]
+    all_heads = jnp.roll(out, places, axis=1)
     out_full, kv_full = (
         lax.all_gather(out_weight, "seq", axis=0, tiled=True),
         lax.all_gather(kv_weight, "seq", axis=0, tiled=True),

time: 393 us -> 350 us (0.89)
  waiting for transfers between devices: 280 us -> 211 us
  starting transfers between devices: 0.2 us -> 15.3 us
  local copies, waits for them, and re-layouts: 4.19 us -> 16.4 us
    all_gather x1, waiting for transfers between devices: 64.4 us -> 0.01 us  [on_device(): lax.all_gather(out_weight, 'seq', axis=0, tiled=True)]
    ppermute x0 -> x7, waiting for transfers between devices: none -> 57.8 us  [on_device(): pieces = [lax.ppermute(pieces[0], 'head', right), *pieces]]
    all_gather x1 -> x0, waiting for transfers between devices: 43.4 us -> none  [on_device(): all_heads = lax.all_gather(mixed, 'head', axis=1, tiled=True)]
    all_gather x1, waiting for transfers between devices: 63.8 us -> 44.5 us  [on_device(): lax.all_gather(kv_weight, 'seq', axis=0, tiled=True)]
    ppermute x0 -> x7, starting transfers between devices: none -> 15.1 us  [on_device(): pieces = [lax.ppermute(pieces[0], 'head', right), *pieces]]
    unnamed x13 -> x28, local copies, waits for them, and re-layouts: 1.51 us -> 12.9 us
  transfers between devices with their start and end apart: 5 -> 11, of which waited for: 5 -> 10; matrix products, arithmetic and copies ran while one was open for 6% -> 11% of each run, Pallas kernels for 0% -> 0%
where the time goes in v1:
time: 350 us; the launch traced here: 347 us
  waiting for transfers between devices  211 us (60%)
  blocking collectives  59.6 us (17%)
  other arithmetic  19.5 us (6%)
  local copies, waits for them, and re-layouts  16.4 us (5%)
  starting transfers between devices  15.3 us (4%)
  between operations  14 us (4%)
  matrix products  11.3 us (3%)
    all_gather x1, waiting for transfers between devices, entering(): gathered = jax.tree.map(lambda a: lax.all_gather(a, axis), part)  63.1 us
    ppermute x7, waiting for transfers between devices, on_device(): pieces = [lax.ppermute(pieces[0], 'head', right), *pieces]  57.8 us
    all_gather x1, waiting for transfers between devices, on_device(): normalized = lax.all_gather(local_norm, 'head', axis=1, tiled=True)  44.8 us
    all_gather x1, blocking collectives, entering(): gathered = jax.tree.map(lambda a: lax.all_gather(a, axis), part)  44.7 us
    all_gather x1, waiting for transfers between devices, on_device(): lax.all_gather(kv_weight, 'seq', axis=0, tiled=True)  44.5 us
    add x16, other arithmetic, combine_states(): later[0][:, None, None] * earlier[1] + later[1]  17 us
    ppermute x7, starting transfers between devices, on_device(): pieces = [lax.ppermute(pieces[0], 'head', right), *pieces]  15.1 us
    psum x1, blocking collectives, on_device(): squares = lax.psum(jnp.sum(wide * wide, axis=1), 'head')  14.8 us
  transfers between devices with their start and end apart: 11, of which 10 were waited for; matrix products, arithmetic and copies ran while one was open for 11% of the time, Pallas kernels for 0%

profile of v1, /device:TPU:2, one launch (start us, length us, event | category | flops | bytes accessed | tf_op | source)
XLA Modules:
  0.0 347.5 jit_solution(66699067743579965)
XLA Ops:
  8.0 1.2 reduce-window.6
  10.9 2.0 convolution_add_fusion
  13.8 44.7 %all-gather.1 = f32[64,1,4]{2,1,0:T(1,128)S(1)} all-gather(f32[1,1,4]{2,1,0:T(1,128)S(1)} %bitcast.96), channel_id=1, replica_groups=mesh['seq'=64,'head'=8] {'seq'}, dimensions={0}, use_global_device_ids=true | all-gather | bytes 1040 | tf_op jit(solution)/shard_map/all_gather | solution.py:11
  59.4 63.1 %all-gather.13.cloned.1.call-done = f32[256,128,128]{2,1,0:T(8,128)} async-done(((f32[4,128,128]{2,1,0:T(8,128)}), f32[256,128,128]{2,1,0:T(8,128)}) %all-gather.13.cloned.1.call-update) | async-done | bytes 16777232 | tf_op jit(solution)/shard_map/all_gather | solution.py:11
  122.5 17.8 %while.3 = (s32[]{:T(128)}, f32[4,128,128]{2,1,0:T(8,128)S(1)}, s32[]{:T(128)}, f32[64,4]{1,0:T(8,128)S(1)}, f32[64,4,128,128]{3,2,1,0:T(8,128)}, /*index=5*/s32[]{:T(128)}, s32[]{:T(128)}, s32[]{:T(128)}) while((s32[]{:T(128)}, f32[4,128,128]{2,1,0:T(8,128)S(1)}, s32[]{:T(128)}, f32[64,4]{1,0:T(8,128)S(1)}, f32[64,4,128,128]{3,2,1,0:T(8,128)}, ...), condition=%wide.region_3.4_spmd, body=%wide.region_2.3_spmd.sunk | while | flops 131077 | bytes 786607 | solution.py:19
  142.0 3.4 collective-permute-start
  145.4 8.6 %collective-permute-done = bf16[256,512]{1,0:T(8,128)(2,1)S(1)} collective-permute-done((bf16[256,512]{1,0:T(8,128)(2,1)S(1)}, bf16[256,512]{1,0:T(8,128)(2,1)S(1)}, u32[]{:S(2)}, u32[]{:S(2)}) %collective-permute-start) | collective-permute-done | bytes 262176 | tf_op jit(solution)/shard_map/ppermute | solution.py:95
  153.9 2.2 collective-permute-start.1
  156.2 9.4 %collective-permute-done.1 = bf16[256,512]{1,0:T(8,128)(2,1)S(1)} collective-permute-done((bf16[256,512]{1,0:T(8,128)(2,1)S(1)}, bf16[256,512]{1,0:T(8,128)(2,1)S(1)}, u32[]{:S(2)}, u32[]{:S(2)}) %collective-permute-start.1) | collective-permute-done | bytes 262176 | tf_op jit(solution)/shard_map/ppermute | solution.py:95
  165.6 1.9 collective-permute-start.2
  167.5 9.0 %collective-permute-done.2 = bf16[256,512]{1,0:T(8,128)(2,1)S(1)} collective-permute-done((bf16[256,512]{1,0:T(8,128)(2,1)S(1)}, bf16[256,512]{1,0:T(8,128)(2,1)S(1)}, u32[]{:S(2)}, u32[]{:S(2)}) %collective-permute-start.2) | collective-permute-done | bytes 262176 | tf_op jit(solution)/shard_map/ppermute | solution.py:95
  176.6 1.9 collective-permute-start.3
  178.5 8.1 %collective-permute-done.3 = bf16[256,512]{1,0:T(8,128)(2,1)S(1)} collective-permute-done((bf16[256,512]{1,0:T(8,128)(2,1)S(1)}, bf16[256,512]{1,0:T(8,128)(2,1)S(1)}, u32[]{:S(2)}, u32[]{:S(2)}) %collective-permute-start.3) | collective-permute-done | bytes 262176 | tf_op jit(solution)/shard_map/ppermute | solution.py:95
  186.6 1.9 collective-permute-start.4
  188.5 7.5 %collective-permute-done.4 = bf16[256,512]{1,0:T(8,128)(2,1)S(1)} collective-permute-done((bf16[256,512]{1,0:T(8,128)(2,1)S(1)}, bf16[256,512]{1,0:T(8,128)(2,1)S(1)}, u32[]{:S(2)}, u32[]{:S(2)}) %collective-permute-start.4) | collective-permute-done | bytes 262176 | tf_op jit(solution)/shard_map/ppermute | solution.py:95
  196.1 1.9 collective-permute-start.5
  198.0 7.5 %collective-permute-done.5 = bf16[256,512]{1,0:T(8,128)(2,1)S(1)} collective-permute-done((bf16[256,512]{1,0:T(8,128)(2,1)S(1)}, bf16[256,512]{1,0:T(8,128)(2,1)S(1)}, u32[]{:S(2)}, u32[]{:S(2)}) %collective-permute-start.5) | collective-permute-done | bytes 262176 | tf_op jit(solution)/shard_map/ppermute | solution.py:95
  205.6 1.9 collective-permute-start.6
  207.5 7.5 %collective-permute-done.6 = bf16[256,512]{1,0:T(8,128)(2,1)S(1)} collective-permute-done((bf16[256,512]{1,0:T(8,128)(2,1)S(1)}, bf16[256,512]{1,0:T(8,128)(2,1)S(1)}, u32[]{:S(2)}, u32[]{:S(2)}) %collective-permute-start.6) | collective-permute-done | bytes 262176 | tf_op jit(solution)/shard_map/ppermute | solution.py:95
  227.2 4.2 %multiply_reduce_fusion = (f32[256]{0:T(256)S(1)}, f32[256,512]{1,0:T(8,128)S(1)}) fusion(bf16[4096,512]{1,0:T(8,128)(2,1)} %all-gather.7.cloned.1.call-done, bf16[256,8192]{1,0:T(8,128)(2,1)} %constant_dynamic-update-slice_fusion, s32[]{:T(128)S(6)} %select_n.34, bf16[256,512]{1,0:T(8,128)(2,1)S(1)} %copy-done.4), kind=kOutput, calls=%fused_computation.24 | convolution fusion | flops 1074528000 | bytes 7078916 | tf_op jit(solution)/shard_map/dot_general | solution.py:103
  231.4 14.8 %psum.7 = f32[256]{0:T(256)S(1)} all-reduce(f32[256]{0:T(256)S(1)} %get-tuple-element.97), channel_id=1, replica_groups=mesh['seq'=64,'head'=8] {'head'}, use_global_device_ids=true, to_apply=%region_6.7 | all-reduce | flops 256 | bytes 2048 | tf_op jit(solution)/shard_map/psum | solution.py:106
  247.1 44.5 %all-gather.11.cloned.1.call-done = bf16[4096,256]{1,0:T(8,128)(2,1)} async-done(((bf16[64,256]{1,0:T(8,128)(2,1)}), bf16[4096,256]{1,0:T(8,128)(2,1)}) %all-gather.11.cloned.1.call-update) | async-done | bytes 2097168 | tf_op jit(solution)/shard_map/all_gather | solution.py:101
  291.5 44.8 %all-gather.9.cloned.1.call-done = bf16[256,4096]{1,0:T(8,128)(2,1)} async-done(((bf16[256,512]{1,0:T(8,128)(2,1)}), bf16[256,4096]{1,0:T(8,128)(2,1)}) %all-gather.9.cloned.1.call-update) | async-done | bytes 2097168 | tf_op jit(solution)/shard_map/all_gather | solution.py:110
  336.3 3.1 convolution_convert_fusion
  (95 shorter events, 37.5 us)
Async XLA Ops:
  7.2 51.4 %copy-start = (bf16[256,512]{1,0:T(8,128)(2,1)S(1)}, bf16[256,512]{1,0:T(8,128)(2,1)}, u32[]{:S(2)}) copy-start(bf16[256,512]{1,0:T(8,128)(2,1)} %param.11) | copy-start | bytes 786436
  7.2 115.3 %all-gather.13.cloned.1.call-start = ((), (), s32[]{:S(2)}) async-start(), calls=%async_computation.3 | async-start | bytes 17039360 | tf_op jit(solution)/shard_map/all_gather | solution.py:11
  13.0 214.2 %all-gather.7.cloned.1.call-start = ((), (), s32[]{:S(2)}) async-start(), calls=%async_computation | async-start | bytes 4259840 | tf_op jit(solution)/shard_map/all_gather | solution.py:100
  13.8 277.8 %all-gather.11.cloned.1.call-start = ((), (), s32[]{:S(2)}) async-start(), calls=%async_computation.2 | async-start | bytes 2129920 | tf_op jit(solution)/shard_map/all_gather | solution.py:101
  58.6 82.2 %copy-start.1 = (bf16[256,512]{1,0:T(8,128)(2,1)S(1)}, bf16[256,512]{1,0:T(8,128)(2,1)}, u32[]{:S(2)}) copy-start(bf16[256,512]{1,0:T(8,128)(2,1)} %param.13) | copy-start | bytes 786436
  122.5 19.3 %copy-start.2 = (bf16[256,512]{1,0:T(8,128)(2,1)S(1)}, bf16[256,512]{1,0:T(8,128)(2,1)}, u32[]{:S(2)}) copy-start(bf16[256,512]{1,0:T(8,128)(2,1)} %param.14) | copy-start | bytes 786436
  140.3 67.2 %copy-start.3 = (bf16[512]{0:T(512)(128)(2,1)S(1)}, bf16[512]{0:T(512)(128)(2,1)}, u32[]{:S(2)}) copy-start(bf16[512]{0:T(512)(128)(2,1)} %param.18) | copy-start | bytes 3076
  142.0 12.0 %collective-permute-start = (bf16[256,512]{1,0:T(8,128)(2,1)S(1)}, bf16[256,512]{1,0:T(8,128)(2,1)S(1)}, u32[]{:S(2)}, u32[]{:S(2)}) collective-permute-start(bf16[256,512]{1,0:T(8,128)(2,1)S(1)} %fusion.21), channel_id=1, source_target_pairs={{0,1},{1,2},{2,3},{3,4},{4,5},{5,6},{6,7},{7,0},{8,9},{9,10},{10,1... | collective-permute-start | bytes 786440 | tf_op jit(solution)/shard_map/ppermute | solution.py:95
  153.9 11.7 %collective-permute-start.1 = (bf16[256,512]{1,0:T(8,128)(2,1)S(1)}, bf16[256,512]{1,0:T(8,128)(2,1)S(1)}, u32[]{:S(2)}, u32[]{:S(2)}) collective-permute-start(bf16[256,512]{1,0:T(8,128)(2,1)S(1)} %collective-permute-done), channel_id=1, source_target_pairs={{0,1},{1,2},{2,3},{3,4},{4,5},{5,6},{6,7},{7,0},{8,9},{9,10},{10,1... | collective-permute-start | bytes 786440 | tf_op jit(solution)/shard_map/ppermute | solution.py:95
  156.1 180.2 %all-gather.9.cloned.1.call-start = ((), (), s32[]{:S(2)}) async-start(), calls=%async_computation.1 | async-start | bytes 2359296 | tf_op jit(solution)/shard_map/all_gather | solution.py:110
  165.6 11.0 %collective-permute-start.2 = (bf16[256,512]{1,0:T(8,128)(2,1)S(1)}, bf16[256,512]{1,0:T(8,128)(2,1)S(1)}, u32[]{:S(2)}, u32[]{:S(2)}) collective-permute-start(bf16[256,512]{1,0:T(8,128)(2,1)S(1)} %collective-permute-done.1), channel_id=1, source_target_pairs={{0,1},{1,2},{2,3},{3,4},{4,5},{5,6},{6,7},{7,0},{8,9},{9,10},{10,1... | collective-permute-start | bytes 786440 | tf_op jit(solution)/shard_map/ppermute | solution.py:95
  176.6 10.1 %collective-permute-start.3 = (bf16[256,512]{1,0:T(8,128)(2,1)S(1)}, bf16[256,512]{1,0:T(8,128)(2,1)S(1)}, u32[]{:S(2)}, u32[]{:S(2)}) collective-permute-start(bf16[256,512]{1,0:T(8,128)(2,1)S(1)} %collective-permute-done.2), channel_id=1, source_target_pairs={{0,1},{1,2},{2,3},{3,4},{4,5},{5,6},{6,7},{7,0},{8,9},{9,10},{10,1... | collective-permute-start | bytes 786440 | tf_op jit(solution)/shard_map/ppermute | solution.py:95
  186.6 9.5 %collective-permute-start.4 = (bf16[256,512]{1,0:T(8,128)(2,1)S(1)}, bf16[256,512]{1,0:T(8,128)(2,1)S(1)}, u32[]{:S(2)}, u32[]{:S(2)}) collective-permute-start(bf16[256,512]{1,0:T(8,128)(2,1)S(1)} %collective-permute-done.3), channel_id=1, source_target_pairs={{0,1},{1,2},{2,3},{3,4},{4,5},{5,6},{6,7},{7,0},{8,9},{9,10},{10,1... | collective-permute-start | bytes 786440 | tf_op jit(solution)/shard_map/ppermute | solution.py:95
  196.1 9.5 %collective-permute-start.5 = (bf16[256,512]{1,0:T(8,128)(2,1)S(1)}, bf16[256,512]{1,0:T(8,128)(2,1)S(1)}, u32[]{:S(2)}, u32[]{:S(2)}) collective-permute-start(bf16[256,512]{1,0:T(8,128)(2,1)S(1)} %collective-permute-done.4), channel_id=1, source_target_pairs={{0,1},{1,2},{2,3},{3,4},{4,5},{5,6},{6,7},{7,0},{8,9},{9,10},{10,1... | collective-permute-start | bytes 786440 | tf_op jit(solution)/shard_map/ppermute | solution.py:95
  205.6 9.5 %collective-permute-start.6 = (bf16[256,512]{1,0:T(8,128)(2,1)S(1)}, bf16[256,512]{1,0:T(8,128)(2,1)S(1)}, u32[]{:S(2)}, u32[]{:S(2)}) collective-permute-start(bf16[256,512]{1,0:T(8,128)(2,1)S(1)} %collective-permute-done.5), channel_id=1, source_target_pairs={{0,1},{1,2},{2,3},{3,4},{4,5},{5,6},{6,7},{7,0},{8,9},{9,10},{10,1... | collective-permute-start | bytes 786440 | tf_op jit(solution)/shard_map/ppermute | solution.py:95
  207.5 19.7 %copy-start.4 = (bf16[256,512]{1,0:T(8,128)(2,1)S(1)}, bf16[256,512]{1,0:T(8,128)(2,1)}, u32[]{:S(2)}) copy-start(bf16[256,512]{1,0:T(8,128)(2,1)} %param.15) | copy-start | bytes 786436
Sparse Core Ops, SparseCore 0:
  13.1 109.3 all-gather.12
  125.8 81.7 all-gather.6
  211.0 80.4 all-gather.10
  293.4 42.8 all-gather.8
